TPU v7x, 128 devices: a whole 4x4x4 slice. The times are simulated.
128 devices in a mesh: gx: 16 (over z, y), gy: 8 (over x, core).
Axes of the slice: x: 4, y: 4, z: 4, core: 2. Of those that a mesh axis runs over, the one named last changes fastest.
Arguments:
- tracers: float32 [8, 16, 4, 36, 64, 128], P('gy', 'gx'), may hold values from -6 to 6
- velocity: float32 [8, 16, 2, 36, 64, 128], P('gy', 'gx'), may hold values from -0.8 to 0.8
- mixing_rate: float32 [8, 16, 35, 64, 128], P('gy', 'gx'), may hold values from 0.05 to 5
- column_depth: float32 [8, 16, 64, 128], P('gy', 'gx'), may hold values from 0.25 to 2.5
- ocean_mask: int32 [8, 28], replicated, may hold values from 0 to 1, as said below
- clinic_list: int32 [8, 16], replicated, may hold values from 0 to 27, as said below
- tropic_list: int32 [8, 32], replicated, may hold values from -1 to 27, as said below
Outputs:
- new_tracers: float32 [8, 16, 4, 36, 64, 128], P('gy', 'gx')
- surface_height: float32 [8, 32, 64, 128], P('gy', 'gx')
Inputs may be any that keep to these rules, and one draw needn't show every extreme that they name: `ocean_mask`: every block row holds exactly 16 ocean blocks. `clinic_list`: row r lists every ocean block column of block row r exactly once. `tropic_list`: row r lists every ocean block column of block row r exactly once and holds -1 elsewhere; the 2 entries of one device are either all -1 or all blocks.
All inputs are finite; a program needn't handle non-finite values.
Results may differ from a plain program's by a relative error of at most 0.0003.
Values sent between devices are 32-bit elements; how exact they have to be, the bound alone decides.
No kernel may reach another device: no remote copies, remote signals or barrier semaphores. Data moves between devices by JAX's collectives and lax.ppermute only.
A program may use at most 128 MiB of HBM per device.

v0:
```python
import jax
import jax.numpy as jnp
from jax import lax
from jax.sharding import PartitionSpec as P

ITERS = 3
diffusion = 0.12
area_term = 0.1
thermal = 0.2
haline = 0.25
cabbeling = 0.05
forcing = 4.0


def passed_along(value, axis, steps):
    count = lax.axis_size(axis)
    leading, last = (max(0, -steps), min(count, count - steps))
    return lax.ppermute(value, axis, [(source, source + steps) for source in range(leading, last)])


def inverse_map(column_list, row_width):
    row_count, slot_count = column_list.shape
    target = jnp.where(column_list < 0, row_width, column_list)
    row_ids = jnp.broadcast_to(
        jnp.arange(row_count, dtype=jnp.int32)[:, None], (row_count, slot_count)
    )
    slot_ids = jnp.broadcast_to(
        jnp.arange(slot_count, dtype=jnp.int32)[None, :], (row_count, slot_count)
    )
    lookup = jnp.zeros((row_count, row_width + 1), jnp.int32).at[row_ids, target].set(slot_ids)
    return lookup[:, :row_width]


def links(columns, row_ids, ocean_mask, inverse):
    row_count, row_width = ocean_mask.shape
    in_use = (columns >= 0).astype(jnp.float32)
    column = jnp.maximum(columns, 0)
    east_col = (column + 1) % row_width
    west_col = (column + row_width - 1) % row_width
    north_row = jnp.minimum(row_ids + 1, row_count - 1)
    south_row = jnp.maximum(row_ids - 1, 0)
    has_north = (row_ids + 1 < row_count).astype(jnp.float32)
    has_south = (row_ids > 0).astype(jnp.float32)
    mask_float = ocean_mask.astype(jnp.float32)
    face_open = (
        in_use * mask_float[row_ids, east_col],
        in_use * mask_float[row_ids, west_col],
        in_use * has_north * mask_float[north_row, column],
        in_use * has_south * mask_float[south_row, column],
    )
    slot_ids = (
        inverse[row_ids, east_col],
        inverse[row_ids, west_col],
        inverse[north_row, column],
        inverse[south_row, column],
    )
    return (face_open, slot_ids)


def divergence(values, speeds, low_side, high_side, low_speed, open_low, open_high, along_axis):
    length = values.shape[along_axis]
    extended = jnp.concatenate(
        [jnp.expand_dims(low_side, along_axis), values, jnp.expand_dims(high_side, along_axis)],
        axis=along_axis,
    )
    face_speed = jnp.concatenate([jnp.expand_dims(low_speed, along_axis), speeds], axis=along_axis)
    behind = lax.slice_in_dim(extended, 0, length + 1, axis=along_axis)
    forward = lax.slice_in_dim(extended, 1, length + 2, axis=along_axis)
    fluxes = face_speed * (0.5 * (behind + forward)) - diffusion * (forward - behind)
    fluxes = jnp.concatenate(
        [
            lax.slice_in_dim(fluxes, 0, 1, axis=along_axis) * open_low,
            lax.slice_in_dim(fluxes, 1, length, axis=along_axis),
            lax.slice_in_dim(fluxes, length, length + 1, axis=along_axis) * open_high,
        ],
        axis=along_axis,
    )
    return lax.slice_in_dim(fluxes, 1, length + 1, axis=along_axis) - lax.slice_in_dim(
        fluxes, 0, length, axis=along_axis
    )


def vertical_mix(stirred, mixing_rate):
    levels = stirred.shape[3]
    coupling = mixing_rate[:, :, None]
    nothing = jnp.zeros_like(coupling[:, :, :, 0])
    interfaces = [coupling[:, :, :, level_index] for level_index in range(levels - 1)]
    above = [nothing] + interfaces
    beneath = interfaces + [nothing]
    factors = []
    partial_sol = []
    for level_index in range(levels):
        diagonal = 1.0 + above[level_index] + beneath[level_index]
        source = stirred[:, :, :, level_index]
        if level_index > 0:
            diagonal = diagonal - above[level_index] * factors[level_index - 1]
            source = source + above[level_index] * partial_sol[level_index - 1]
        factors.append(beneath[level_index] / diagonal)
        partial_sol.append(source / diagonal)
    result_levels = [partial_sol[levels - 1]]
    for level_index in range(levels - 2, -1, -1):
        result_levels.insert(0, partial_sol[level_index] + factors[level_index] * result_levels[0])
    return jnp.stack(result_levels, axis=3)


def tracer_core(tracers, velocity, mixing_rate, halo_values, face_open):
    west_tracer, west_speed, east_tracer, south_tracer, south_speed, north_tracer = halo_values
    open_east, open_west, open_north, open_south = [
        opening[:, :, None, None, None, None] for opening in face_open
    ]
    east_speed = velocity[:, :, 0:1]
    north_speed = velocity[:, :, 1:2]
    stirred = (
        tracers
        - divergence(
            tracers,
            east_speed,
            west_tracer,
            east_tracer,
            west_speed[:, :, None],
            open_west,
            open_east,
            5,
        )
        - divergence(
            tracers,
            north_speed,
            south_tracer,
            north_tracer,
            south_speed[:, :, None],
            open_south,
            open_north,
            4,
        )
    )
    mixed = vertical_mix(stirred, mixing_rate)
    levels = mixed.shape[3]
    spacing = 2.0 * (jnp.arange(levels, dtype=jnp.float32) + 1.0) / (levels * (levels + 1))
    heat = mixed[:, :, 0]
    salinity = mixed[:, :, 1]
    density = haline * salinity - thermal * heat - cabbeling * heat * heat
    column_forcing = forcing * jnp.sum(density * spacing[None, None, :, None, None], axis=2)
    return (mixed, column_forcing)


def face_weights(column_depth, depth_halos, face_open):
    west_depth, east_depth, south_depth, north_depth = depth_halos
    open_east, open_west, open_north, open_south = [
        opening[:, :, None, None] for opening in face_open
    ]
    cells_east = column_depth.shape[3]
    cells_north = column_depth.shape[2]
    edge_east = (jnp.arange(cells_east) == cells_east - 1)[None, None, None, :]
    edge_west = (jnp.arange(cells_east) == 0)[None, None, None, :]
    edge_north = (jnp.arange(cells_north) == cells_north - 1)[None, None, :, None]
    edge_south = (jnp.arange(cells_north) == 0)[None, None, :, None]
    to_east = jnp.concatenate([column_depth[..., 1:], east_depth[..., None]], axis=3)
    to_west = jnp.concatenate([west_depth[..., None], column_depth[..., :-1]], axis=3)
    to_north = jnp.concatenate([column_depth[:, :, 1:], north_depth[:, :, None]], axis=2)
    to_south = jnp.concatenate([south_depth[:, :, None], column_depth[:, :, :-1]], axis=2)
    weight_east = 0.5 * (column_depth + to_east) * jnp.where(edge_east, open_east, 1.0)
    weight_west = 0.5 * (column_depth + to_west) * jnp.where(edge_west, open_west, 1.0)
    weight_north = 0.5 * (column_depth + to_north) * jnp.where(edge_north, open_north, 1.0)
    weight_south = 0.5 * (column_depth + to_south) * jnp.where(edge_south, open_south, 1.0)
    return jnp.stack([weight_east, weight_west, weight_north, weight_south], axis=2)


def apply_operator(values, weights, halo_values):
    east_side, west_side, north_side, south_side = halo_values
    weight_east = weights[:, :, 0]
    weight_west = weights[:, :, 1]
    weight_north = weights[:, :, 2]
    weight_south = weights[:, :, 3]
    to_east = jnp.concatenate([values[..., 1:], east_side[..., None]], axis=3)
    to_west = jnp.concatenate([west_side[..., None], values[..., :-1]], axis=3)
    to_north = jnp.concatenate([values[:, :, 1:], north_side[:, :, None]], axis=2)
    to_south = jnp.concatenate([south_side[:, :, None], values[:, :, :-1]], axis=2)
    return (
        (area_term + weight_east + weight_west + weight_north + weight_south) * values
        - weight_east * to_east
        - weight_west * to_west
        - weight_north * to_north
        - weight_south * to_south
    )


def picked(band_rows, slot_ids):
    return jnp.take(band_rows[0], slot_ids[0], axis=0)[None]


def exchange_edges(values, slot_ids):
    slot_east, slot_west, slot_north, slot_south = slot_ids
    cells_north = values.shape[2]
    side_cols = jnp.concatenate([values[..., -1], values[..., 0]], axis=2)
    from_below = passed_along(values[:, :, -1, :], "gy", 1)
    from_above = passed_along(values[:, :, 0, :], "gy", -1)
    band_sides, band_below, band_above = (
        lax.all_gather(side_cols, "gx", axis=1, tiled=True),
        lax.all_gather(from_below, "gx", axis=1, tiled=True),
        lax.all_gather(from_above, "gx", axis=1, tiled=True),
    )
    return (
        picked(band_sides, slot_east)[..., cells_north:],
        picked(band_sides, slot_west)[..., :cells_north],
        picked(band_above, slot_north),
        picked(band_below, slot_south),
    )


def squares(residual):
    return lax.psum(jnp.sum(residual * residual), ("gx", "gy"))


def solve(forcing_field, weights, slot_ids):
    solution = jnp.zeros_like(forcing_field)
    residual = forcing_field
    direction = forcing_field
    norm_now = squares(residual)
    for iteration in range(ITERS):
        image_field = apply_operator(direction, weights, exchange_edges(direction, slot_ids))
        step_size = norm_now / lax.psum(jnp.sum(direction * image_field), ("gx", "gy"))
        solution = solution + step_size * direction
        if iteration + 1 < ITERS:
            residual = residual - step_size * image_field
            norm_next = squares(residual)
            direction = residual + norm_next / norm_now * direction
            norm_now = norm_next
    return solution


def body(tracers, velocity, mixing_rate, column_depth, ocean_mask, clinic_list, tropic_list):
    band_row = lax.axis_index("gy")
    band_col = lax.axis_index("gx")
    slot_count = tracers.shape[1]
    tracer_count = tracers.shape[2]
    levels = tracers.shape[3]
    cells_north = tracers.shape[4]
    cells_east = tracers.shape[5]
    row_width = ocean_mask.shape[1]
    inverse = inverse_map(clinic_list, row_width)
    clinic_row = lax.dynamic_index_in_dim(clinic_list, band_row, 0, keepdims=False)
    own_columns = lax.dynamic_slice_in_dim(clinic_row, band_col * slot_count, slot_count)[None]
    row_ids = jnp.full((1, slot_count), band_row, jnp.int32)
    face_open, slot_ids = links(own_columns, row_ids, ocean_mask, inverse)
    slot_east, slot_west, slot_north, slot_south = slot_ids
    east_cols = jnp.concatenate(
        [
            tracers[..., -1].reshape(1, slot_count, -1),
            velocity[:, :, 0, :, :, -1].reshape(1, slot_count, -1),
            column_depth[..., -1],
        ],
        axis=2,
    )
    west_cols = jnp.concatenate(
        [tracers[..., 0].reshape(1, slot_count, -1), column_depth[..., 0]], axis=2
    )
    side_cols = jnp.concatenate([east_cols, west_cols], axis=2)
    north_rows = jnp.concatenate(
        [
            tracers[..., -1, :].reshape(1, slot_count, -1),
            velocity[:, :, 1, :, -1, :].reshape(1, slot_count, -1),
            column_depth[..., -1, :],
        ],
        axis=2,
    )
    south_rows = jnp.concatenate(
        [tracers[..., 0, :].reshape(1, slot_count, -1), column_depth[..., 0, :]], axis=2
    )
    band_sides, band_north, band_south = (
        lax.all_gather(side_cols, "gx", axis=1, tiled=True),
        lax.all_gather(north_rows, "gx", axis=1, tiled=True),
        lax.all_gather(south_rows, "gx", axis=1, tiled=True),
    )
    band_below = passed_along(band_north, "gy", 1)
    band_above = passed_along(band_south, "gy", -1)
    tracer_len = tracer_count * levels
    east_len = (tracer_len + levels + 1) * cells_north
    from_west = picked(band_sides, slot_west)[..., :east_len]
    from_east = picked(band_sides, slot_east)[..., east_len:]
    from_south = picked(band_below, slot_south)
    from_north = picked(band_above, slot_north)
    halo_values = (
        from_west[..., : tracer_len * cells_north].reshape(
            1, slot_count, tracer_count, levels, cells_north
        ),
        from_west[..., tracer_len * cells_north : (tracer_len + levels) * cells_north].reshape(
            1, slot_count, levels, cells_north
        ),
        from_east[..., : tracer_len * cells_north].reshape(
            1, slot_count, tracer_count, levels, cells_north
        ),
        from_south[..., : tracer_len * cells_east].reshape(
            1, slot_count, tracer_count, levels, cells_east
        ),
        from_south[..., tracer_len * cells_east : (tracer_len + levels) * cells_east].reshape(
            1, slot_count, levels, cells_east
        ),
        from_north[..., : tracer_len * cells_east].reshape(
            1, slot_count, tracer_count, levels, cells_east
        ),
    )
    depth_halos = (
        from_west[..., (tracer_len + levels) * cells_north :],
        from_east[..., tracer_len * cells_north :],
        from_south[..., (tracer_len + levels) * cells_east :],
        from_north[..., tracer_len * cells_east :],
    )
    new_tracers, column_forcing = tracer_core(
        tracers, velocity, mixing_rate, halo_values, face_open
    )
    weights = face_weights(column_depth, depth_halos, face_open)
    tropic_row = lax.dynamic_index_in_dim(tropic_list, band_row, 0, keepdims=False)
    tropic_count = tropic_list.shape[1] // lax.axis_size("gx")
    own_tropic = lax.dynamic_slice_in_dim(tropic_row, band_col * tropic_count, tropic_count)[None]
    in_use = (own_tropic >= 0)[:, :, None, None]
    inverse_row = lax.dynamic_index_in_dim(inverse, band_row, 0, keepdims=False)
    source_slot = jnp.take(inverse_row, jnp.maximum(own_tropic, 0), axis=0)
    packed = jnp.concatenate([column_forcing[:, :, None], weights], axis=2)
    band_fields = lax.all_gather(packed, "gx", axis=1, tiled=True)
    moved = jnp.where(in_use[..., None], picked(band_fields, source_slot), 0.0)
    tropic_inverse = inverse_map(tropic_list, row_width)
    tropic_ids = jnp.full((1, tropic_count), band_row, jnp.int32)
    tropic_slots = links(own_tropic, tropic_ids, ocean_mask, tropic_inverse)[1]
    surface_height = solve(moved[:, :, 0], moved[:, :, 1:], tropic_slots)
    return (new_tracers, surface_height)


def solution(mesh):
    return jax.shard_map(
        body,
        mesh=mesh,
        in_specs=(
            P("gy", "gx", None, None, None, None),
            P("gy", "gx", None, None, None, None),
            P("gy", "gx", None, None, None),
            P("gy", "gx", None, None),
            P(),
            P(),
            P(),
        ),
        out_specs=(P("gy", "gx", None, None, None, None), P("gy", "gx", None, None)),
        check_vma=False,
    )
```

profile of v0, /device:TPU:1, one launch (start us, length us, event | category | flops | bytes accessed | tf_op | source)
XLA Modules:
  0.0 796.5 jit_solution(15573469216887903358)
XLA Ops:
  10.1 7.6 slice_reduce_fusion
  20.7 5.3 constant_dynamic-update-slice_fusion.1
  30.4 6.4 scatter_fusion
  36.7 5.6 fusion.188
  56.2 5.6 fusion.187
  68.2 32.6 %all-gather.5.cloned.1.call-done = f32[1,16,20864]{2,0,1:T(1,128)} async-done(((f32[1,1,20864]{2,0,1:T(1,128)}), f32[1,16,20864]{2,0,1:T(1,128)}) %all-gather.5.cloned.1.call-update) | async-done | bytes 1335312 | tf_op jit(solution)/shard_map/all_gather | solution.py:270
  102.6 6.8 concatenate.612
  109.5 6.9 concatenate.611
  124.6 5.6 multiply_subtract_fusion
  135.5 9.8 %slice_multiply_fusion = (f32[1,1,4,36,64,1]{5,4,3,2,1,0:T(8,128)}, f32[1,1,4,36,64,1]{5,4,3,2,1,0:T(8,128)}) fusion(f32[1,1,4,36,64,129]{5,4,3,2,1,0:T(8,128)} %copy-done, f32[]{:T(128)} %bitcast.22, f32[]{:T(128)} %bitcast.21), kind=kLoop, calls=%fused_computation.25 | loop fusion | flops 18432 | bytes 147464 | tf_op jit(solution)/shard_map/mul | solution.py:72
  147.0 4.7 collective-permute-start
  152.7 15.5 %collective-permute-done = f32[1,16,23168]{2,0,1:T(1,128)S(1)} collective-permute-done((f32[1,16,23168]{2,0,1:T(1,128)}, f32[1,16,23168]{2,0,1:T(1,128)S(1)}, u32[]{:S(2)}, u32[]{:S(2)}) %collective-permute-start) | collective-permute-done | bytes 1482784 | tf_op jit(solution)/shard_map/ppermute | solution.py:18
  168.5 4.6 multiply_subtract_fusion.1
  176.5 9.6 %fusion.1 = f32[1,1,4,36,64,128]{5,4,3,2,1,0:T(8,128)S(1)} fusion(f32[1,1,4,36,64,128]{5,4,3,2,1,0:T(8,128)S(1)} %bitcast.678, f32[1,1,4,36,64,1]{5,4,3,2,1,0:T(8,128)} %get-tuple-element.253, f32[1,1,4,36,64,127]{5,4,3,2,1,0:T(8,128)S(1)} %bitcast.680, f32[1,1,4,36,64,1]{5,4,3,2,1,0:T(8,128)} %get-tuple-element.252, ...), kind=kLoop, calls=%fused_computation.29 | loop fusion | flops 9437184 | bytes 18984960 | tf_op jit(solution)/shard_map/sub | solution.py:114
  193.9 11.2 %scatter_fusion.1 = s32[8,29]{1,0:T(8,128)S(1)} fusion(s32[8,29]{1,0:T(8,128)S(1)} %broadcast.10948.clone.1, s32[256]{0:T(256)S(1)} %reshape.20049, s32[256]{0:T(256)S(1)} %reshape.20051), kind=kCustom, calls=%fused_computation.19 | custom fusion | bytes 5120 | tf_op jit(solution)/shard_map/scatter | solution.py:30
  208.7 31.2 %all-gather.11.cloned.1.call-done = f32[1,16,5,64,128]{4,3,2,0,1:T(8,128)} async-done(((f32[1,1,5,64,128]{4,3,2,0,1:T(8,128)}), f32[1,16,5,64,128]{4,3,2,0,1:T(8,128)}) %all-gather.11.cloned.1.call-update) | async-done | bytes 2621456 | tf_op jit(solution)/shard_map/all_gather | solution.py:319
  248.6 17.1 %all_gather.43 = f32[1,32,128]{2,0,1:T(1,128)S(1)} all-gather(f32[1,2,128]{2,0,1:T(1,128)S(1)} %bitcast.718), channel_id=1, replica_groups=mesh['gx'=16,'gy'=8] {'gx'}, dimensions={1}, use_global_device_ids=true | all-gather | bytes 17408 | tf_op jit(solution)/shard_map/all_gather | solution.py:198
  267.3 16.0 %all_gather.45 = f32[1,32,128]{2,0,1:T(1,128)S(1)} all-gather(f32[1,2,128]{2,0,1:T(1,128)S(1)} %bitcast.724), channel_id=1, replica_groups=mesh['gx'=16,'gy'=8] {'gx'}, dimensions={1}, use_global_device_ids=true | all-gather | bytes 17408 | tf_op jit(solution)/shard_map/all_gather | solution.py:199
  283.3 17.3 %all_gather.44 = f32[1,32,128]{2,0,1:T(1,128)S(1)} all-gather(f32[1,2,128]{2,0,1:T(1,128)S(1)} %bitcast.723), channel_id=1, replica_groups=mesh['gx'=16,'gy'=8] {'gx'}, dimensions={1}, use_global_device_ids=true | all-gather | bytes 17408 | tf_op jit(solution)/shard_map/all_gather | solution.py:200
  302.5 78.7 %all-reduce.4 = (f32[]{:T(128)}, f32[]{:T(128)}) all-reduce(f32[]{:T(128)} %get-tuple-element.130, f32[]{:T(128)} %get-tuple-element.129), channel_id=1, replica_groups=mesh['gx'=16,'gy'=8] {'gx','gy'}, use_global_device_ids=true, to_apply=%region_3.5 | all-reduce | flops 2 | bytes 16 | tf_op jit(solution)/shard_map/psum | solution.py:211
  383.1 64.1 %psum.44 = f32[]{:T(128)} all-reduce(f32[]{:T(128)} %get-tuple-element.143), channel_id=1, replica_groups=mesh['gx'=16,'gy'=8] {'gx','gy'}, use_global_device_ids=true, to_apply=%region_8.11 | all-reduce | flops 1 | bytes 8 | tf_op jit(solution)/shard_map/psum | solution.py:211
  448.8 15.5 %all_gather.46 = f32[1,32,128]{2,0,1:T(1,128)S(1)} all-gather(f32[1,2,128]{2,0,1:T(1,128)S(1)} %bitcast.719), channel_id=1, replica_groups=mesh['gx'=16,'gy'=8] {'gx'}, dimensions={1}, use_global_device_ids=true | all-gather | bytes 17408 | tf_op jit(solution)/shard_map/all_gather | solution.py:198
  465.5 9.1 %collective-permute-start.5 = (f32[1,2,128]{2,1,0:T(2,128)S(1)}, f32[1,2,128]{2,1,0:T(2,128)S(1)}, u32[]{:S(2)}, u32[]{:S(2)}) collective-permute-start(f32[1,2,128]{2,1,0:T(2,128)S(1)} %bitcast.733), channel_id=1, source_target_pairs={{0,1},{1,2},{2,3},{3,4},{4,5},{5,6},{6,7},{8,9},{9,10},{10,11},{11... | collective-permute-start | bytes 3080 | tf_op jit(solution)/shard_map/ppermute | solution.py:18
  477.0 16.0 %all_gather.48 = f32[1,32,128]{2,0,1:T(1,128)S(1)} all-gather(f32[1,2,128]{2,0,1:T(1,128)S(1)} %bitcast.726), channel_id=1, replica_groups=mesh['gx'=16,'gy'=8] {'gx'}, dimensions={1}, use_global_device_ids=true | all-gather | bytes 17408 | tf_op jit(solution)/shard_map/all_gather | solution.py:199
  493.6 17.0 %all_gather.47 = f32[1,32,128]{2,0,1:T(1,128)S(1)} all-gather(f32[1,2,128]{2,0,1:T(1,128)S(1)} %bitcast.725), channel_id=1, replica_groups=mesh['gx'=16,'gy'=8] {'gx'}, dimensions={1}, use_global_device_ids=true | all-gather | bytes 17408 | tf_op jit(solution)/shard_map/all_gather | solution.py:200
  511.9 73.0 %psum.45 = f32[]{:T(128)} all-reduce(f32[]{:T(128)} %get-tuple-element.141), channel_id=1, replica_groups=mesh['gx'=16,'gy'=8] {'gx','gy'}, use_global_device_ids=true, to_apply=%region_10.13 | all-reduce | flops 1 | bytes 8 | tf_op jit(solution)/shard_map/psum | solution.py:221
  586.9 64.5 %psum.46 = f32[]{:T(128)} all-reduce(f32[]{:T(128)} %multiply_reduce_fusion), channel_id=1, replica_groups=mesh['gx'=16,'gy'=8] {'gx','gy'}, use_global_device_ids=true, to_apply=%region_12.15 | all-reduce | flops 1 | bytes 8 | tf_op jit(solution)/shard_map/psum | solution.py:211
  653.0 15.6 %all_gather.49 = f32[1,32,128]{2,0,1:T(1,128)S(1)} all-gather(f32[1,2,128]{2,0,1:T(1,128)S(1)} %bitcast.720), channel_id=1, replica_groups=mesh['gx'=16,'gy'=8] {'gx'}, dimensions={1}, use_global_device_ids=true | all-gather | bytes 17408 | tf_op jit(solution)/shard_map/all_gather | solution.py:198
  670.1 7.8 collective-permute-start.6
  681.5 16.4 %all_gather.50 = f32[1,32,128]{2,0,1:T(1,128)S(1)} all-gather(f32[1,2,128]{2,0,1:T(1,128)S(1)} %bitcast.728), channel_id=1, replica_groups=mesh['gx'=16,'gy'=8] {'gx'}, dimensions={1}, use_global_device_ids=true | all-gather | bytes 17408 | tf_op jit(solution)/shard_map/all_gather | solution.py:200
  698.5 16.3 %all_gather.51 = f32[1,32,128]{2,0,1:T(1,128)S(1)} all-gather(f32[1,2,128]{2,0,1:T(1,128)S(1)} %bitcast.727), channel_id=1, replica_groups=mesh['gx'=16,'gy'=8] {'gx'}, dimensions={1}, use_global_device_ids=true | all-gather | bytes 17408 | tf_op jit(solution)/shard_map/all_gather | solution.py:199
  716.1 71.9 %psum.47 = f32[]{:T(128)} all-reduce(f32[]{:T(128)} %fusion.60), channel_id=1, replica_groups=mesh['gx'=16,'gy'=8] {'gx','gy'}, use_global_device_ids=true, to_apply=%region_14.17 | all-reduce | flops 1 | bytes 8 | tf_op jit(solution)/shard_map/psum | solution.py:221
  (328 shorter events, 77.6 us)
Async XLA Ops:
  7.2 57.4 %all-gather.9.cloned.1.call-start = ((), (), s32[]{:S(2)}) async-start(), calls=%async_computation.2 | async-start | bytes 1262080 | tf_op jit(solution)/shard_map/all_gather | solution.py:272
  10.0 90.8 %all-gather.5.cloned.1.call-start = ((), (), s32[]{:S(2)}) async-start(), calls=%async_computation | async-start | bytes 1418752 | tf_op jit(solution)/shard_map/all_gather | solution.py:270
  19.9 127.2 %all-gather.7.cloned.1.call-start = ((), (), s32[]{:S(2)}) async-start(), calls=%async_computation.1 | async-start | bytes 1575424 | tf_op jit(solution)/shard_map/all_gather | solution.py:271
  20.7 219.2 %all-gather.11.cloned.1.call-start = ((), (), s32[]{:S(2)}) async-start(), calls=%async_computation.3 | async-start | bytes 2785280 | tf_op jit(solution)/shard_map/all_gather | solution.py:319
  30.4 21.9 %copy-start.4 = (f32[1,1,35,64,128]{4,3,2,1,0:T(8,128)S(1)}, f32[1,1,35,64,128]{4,3,2,1,0:T(8,128)}, u32[]{:S(2)}) copy-start(f32[1,1,35,64,128]{4,3,2,1,0:T(8,128)} %param.13) | copy-start | bytes 3440644
  46.1 10.1 %copy-start.46 = (s32[8,28]{1,0:T(8,128)S(1)}, s32[8,28]{1,0:T(8,128)}, u32[]{:S(2)}) copy-start(s32[8,28]{1,0:T(8,128)} %param.15) | copy-start | bytes 2692
  64.6 87.1 %collective-permute-start.1 = (f32[1,16,18560]{2,0,1:T(1,128)}, f32[1,16,18560]{2,0,1:T(1,128)}, u32[]{:S(2)}, u32[]{:S(2)}) collective-permute-start(f32[1,16,18560]{2,0,1:T(1,128)} %all-gather.9.cloned.1.call-done), channel_id=1, source_target_pairs={{1,0},{2,1},{3,2},{4,3},{5,4},{6,5},{7,6},{9,8},{10,9},{11,10},{12... | collective-permute-start | bytes 3563528 | tf_op jit(solution)/shard_map/ppermute | solution.py:18
  102.6 14.9 %copy-start.6 = (f32[1,1,1,36,64,128]{5,4,3,2,1,0:T(8,128)S(1)}, f32[1,1,1,36,64,128]{5,4,3,2,1,0:T(8,128)}, u32[]{:S(2)}) copy-start(f32[1,1,1,36,64,128]{5,4,3,2,1,0:T(8,128)} %get-tuple-element.259) | copy-start | bytes 3538948
  135.5 32.8 %copy-start.5 = (f32[1,1,1,36,64,128]{5,4,3,2,1,0:T(8,128)S(1)}, f32[1,1,1,36,64,128]{5,4,3,2,1,0:T(8,128)}, u32[]{:S(2)}) copy-start(f32[1,1,1,36,64,128]{5,4,3,2,1,0:T(8,128)} %get-tuple-element.258) | copy-start | bytes 3538948
  147.0 21.2 %collective-permute-start = (f32[1,16,23168]{2,0,1:T(1,128)}, f32[1,16,23168]{2,0,1:T(1,128)S(1)}, u32[]{:S(2)}, u32[]{:S(2)}) collective-permute-start(f32[1,16,23168]{2,0,1:T(1,128)} %all-gather.7.cloned.1.call-done), channel_id=1, source_target_pairs={{0,1},{1,2},{2,3},{3,4},{4,5},{5,6},{6,7},{8,9},{9,10},{10,11},{11... | collective-permute-start | bytes 4448264 | tf_op jit(solution)/shard_map/ppermute | solution.py:18
  176.1 9.9 %copy-start.9 = (f32[64,128]{1,0:T(8,128)S(1)}, f32[64,128]{1,0:T(8,128)}, u32[]{:S(2)}) copy-start(f32[64,128]{1,0:T(8,128)} %get-tuple-element.263) | copy-start | bytes 98308
  176.1 9.9 %copy-start.10 = (f32[64,128]{1,0:T(8,128)S(1)}, f32[64,128]{1,0:T(8,128)}, u32[]{:S(2)}) copy-start(f32[64,128]{1,0:T(8,128)} %get-tuple-element.183) | copy-start | bytes 98308
  176.2 9.9 %copy-start.11 = (f32[64,128]{1,0:T(8,128)S(1)}, f32[64,128]{1,0:T(8,128)}, u32[]{:S(2)}) copy-start(f32[64,128]{1,0:T(8,128)} %get-tuple-element.188) | copy-start | bytes 98308
  176.2 9.9 %copy-start.12 = (f32[64,128]{1,0:T(8,128)S(1)}, f32[64,128]{1,0:T(8,128)}, u32[]{:S(2)}) copy-start(f32[64,128]{1,0:T(8,128)} %get-tuple-element.192) | copy-start | bytes 98308
  176.2 9.9 %copy-start.13 = (f32[64,128]{1,0:T(8,128)S(1)}, f32[64,128]{1,0:T(8,128)}, u32[]{:S(2)}) copy-start(f32[64,128]{1,0:T(8,128)} %get-tuple-element.196) | copy-start | bytes 98308
  176.2 9.9 %copy-start.14 = (f32[64,128]{1,0:T(8,128)S(1)}, f32[64,128]{1,0:T(8,128)}, u32[]{:S(2)}) copy-start(f32[64,128]{1,0:T(8,128)} %get-tuple-element.200) | copy-start | bytes 98308
  176.2 9.9 %copy-start.15 = (f32[64,128]{1,0:T(8,128)S(1)}, f32[64,128]{1,0:T(8,128)}, u32[]{:S(2)}) copy-start(f32[64,128]{1,0:T(8,128)} %get-tuple-element.204) | copy-start | bytes 98308
  176.2 9.9 %copy-start.16 = (f32[64,128]{1,0:T(8,128)S(1)}, f32[64,128]{1,0:T(8,128)}, u32[]{:S(2)}) copy-start(f32[64,128]{1,0:T(8,128)} %get-tuple-element.208) | copy-start | bytes 98308
  176.2 9.9 %copy-start.17 = (f32[64,128]{1,0:T(8,128)S(1)}, f32[64,128]{1,0:T(8,128)}, u32[]{:S(2)}) copy-start(f32[64,128]{1,0:T(8,128)} %get-tuple-element.212) | copy-start | bytes 98308
  176.2 9.9 %copy-start.18 = (f32[64,128]{1,0:T(8,128)S(1)}, f32[64,128]{1,0:T(8,128)}, u32[]{:S(2)}) copy-start(f32[64,128]{1,0:T(8,128)} %get-tuple-element.216) | copy-start | bytes 98308
  176.2 9.9 %copy-start.19 = (f32[64,128]{1,0:T(8,128)S(1)}, f32[64,128]{1,0:T(8,128)}, u32[]{:S(2)}) copy-start(f32[64,128]{1,0:T(8,128)} %get-tuple-element.220) | copy-start | bytes 98308
  176.2 9.9 %copy-start.20 = (f32[64,128]{1,0:T(8,128)S(1)}, f32[64,128]{1,0:T(8,128)}, u32[]{:S(2)}) copy-start(f32[64,128]{1,0:T(8,128)} %get-tuple-element.224) | copy-start | bytes 98308
  176.3 9.9 %copy-start.21 = (f32[64,128]{1,0:T(8,128)S(1)}, f32[64,128]{1,0:T(8,128)}, u32[]{:S(2)}) copy-start(f32[64,128]{1,0:T(8,128)} %get-tuple-element.228) | copy-start | bytes 98308
  176.3 9.9 %copy-start.22 = (f32[64,128]{1,0:T(8,128)S(1)}, f32[64,128]{1,0:T(8,128)}, u32[]{:S(2)}) copy-start(f32[64,128]{1,0:T(8,128)} %get-tuple-element.232) | copy-start | bytes 98308
  176.3 9.9 %copy-start.23 = (f32[64,128]{1,0:T(8,128)S(1)}, f32[64,128]{1,0:T(8,128)}, u32[]{:S(2)}) copy-start(f32[64,128]{1,0:T(8,128)} %get-tuple-element.236) | copy-start | bytes 98308
  176.3 9.9 %copy-start.24 = (f32[64,128]{1,0:T(8,128)S(1)}, f32[64,128]{1,0:T(8,128)}, u32[]{:S(2)}) copy-start(f32[64,128]{1,0:T(8,128)} %get-tuple-element.240) | copy-start | bytes 98308
  242.6 24.6 %collective-permute-start.3 = (f32[1,2,128]{2,1,0:T(2,128)S(1)}, f32[1,2,128]{2,1,0:T(2,128)S(1)}, u32[]{:S(2)}, u32[]{:S(2)}) collective-permute-start(f32[1,2,128]{2,1,0:T(2,128)S(1)} %bitcast.731), channel_id=1, source_target_pairs={{0,1},{1,2},{2,3},{3,4},{4,5},{5,6},{6,7},{8,9},{9,10},{10,11},{11... | collective-permute-start | bytes 3080 | tf_op jit(solution)/shard_map/ppermute | solution.py:18
  246.6 36.6 %collective-permute-start.2 = (f32[1,2,128]{2,1,0:T(2,128)S(1)}, f32[1,2,128]{2,1,0:T(2,128)S(1)}, u32[]{:S(2)}, u32[]{:S(2)}) collective-permute-start(f32[1,2,128]{2,1,0:T(2,128)S(1)} %bitcast.730), channel_id=1, source_target_pairs={{1,0},{2,1},{3,2},{4,3},{5,4},{6,5},{7,6},{9,8},{10,9},{11,10},{12... | collective-permute-start | bytes 3080 | tf_op jit(solution)/shard_map/ppermute | solution.py:18
  465.5 11.5 %collective-permute-start.5 = (f32[1,2,128]{2,1,0:T(2,128)S(1)}, f32[1,2,128]{2,1,0:T(2,128)S(1)}, u32[]{:S(2)}, u32[]{:S(2)}) collective-permute-start(f32[1,2,128]{2,1,0:T(2,128)S(1)} %bitcast.733), channel_id=1, source_target_pairs={{0,1},{1,2},{2,3},{3,4},{4,5},{5,6},{6,7},{8,9},{9,10},{10,11},{11... | collective-permute-start | bytes 3080 | tf_op jit(solution)/shard_map/ppermute | solution.py:18
  474.6 19.0 %collective-permute-start.4 = (f32[1,2,128]{2,1,0:T(2,128)S(1)}, f32[1,2,128]{2,1,0:T(2,128)S(1)}, u32[]{:S(2)}, u32[]{:S(2)}) collective-permute-start(f32[1,2,128]{2,1,0:T(2,128)S(1)} %bitcast.729), channel_id=1, source_target_pairs={{1,0},{2,1},{3,2},{4,3},{5,4},{6,5},{7,6},{9,8},{10,9},{11,10},{12... | collective-permute-start | bytes 3080 | tf_op jit(solution)/shard_map/ppermute | solution.py:18
  670.1 11.4 %collective-permute-start.6 = (f32[1,2,128]{2,1,0:T(2,128)S(1)}, f32[1,2,128]{2,1,0:T(2,128)S(1)}, u32[]{:S(2)}, u32[]{:S(2)}) collective-permute-start(f32[1,2,128]{2,1,0:T(2,128)S(1)} %bitcast.734), channel_id=1, source_target_pairs={{1,0},{2,1},{3,2},{4,3},{5,4},{6,5},{7,6},{9,8},{10,9},{11,10},{12... | collective-permute-start | bytes 3080 | tf_op jit(solution)/shard_map/ppermute | solution.py:18
  678.1 20.5 %collective-permute-start.7 = (f32[1,2,128]{2,1,0:T(2,128)S(1)}, f32[1,2,128]{2,1,0:T(2,128)S(1)}, u32[]{:S(2)}, u32[]{:S(2)}) collective-permute-start(f32[1,2,128]{2,1,0:T(2,128)S(1)} %bitcast.732), channel_id=1, source_target_pairs={{0,1},{1,2},{2,3},{3,4},{4,5},{5,6},{6,7},{8,9},{9,10},{10,11},{11... | collective-permute-start | bytes 3080 | tf_op jit(solution)/shard_map/ppermute | solution.py:18
  (33 other events, 258.6 us)
Sparse Core Ops, SparseCore 0:
  10.1 45.1 all-gather.8
  58.1 42.7 all-gather.4
  103.0 43.9 all-gather.6
  193.9 46.0 all-gather.10
where the time goes:
time: 798 us; the launch traced here: 797 us
  blocking collectives  499 us (63%)
  local copies, waits for them, and re-layouts  101 us (13%)
  waiting for transfers between devices  81.1 us (10%)
  other arithmetic  45.1 us (6%)
  starting transfers between devices  36.4 us (5%)
  between operations  33.6 us (4%)
    psum x3, blocking collectives, squares(): return lax.psum(jnp.sum(residual * residual), ('gx', 'gy'))  207 us
    psum x2, blocking collectives, solve(): lax.psum(jnp.sum(direction * image_field), ('gx', 'gy'))  145 us
    all_gather x3, blocking collectives, exchange_edges(): lax.all_gather(from_above, 'gx', axis=1, tiled=True)  50.7 us
    all_gather x3, blocking collectives, exchange_edges(): lax.all_gather(side_cols, 'gx', axis=1, tiled=True)  48.3 us
    all_gather x3, blocking collectives, exchange_edges(): lax.all_gather(from_below, 'gx', axis=1, tiled=True)  48.2 us
    ppermute x8, starting transfers between devices, passed_along(): lax.ppermute(value, axis, [(source, source + steps) for source in range(l...  36.3 us
    all_gather x1, waiting for transfers between devices, body(): lax.all_gather(side_cols, 'gx', axis=1, tiled=True)  32.6 us
    all_gather x1, waiting for transfers between devices, body(): band_fields = lax.all_gather(packed, 'gx', axis=1, tiled=True)  31.2 us
  transfers between devices with their start and end apart: 12, of which 4 were waited for; matrix products, arithmetic and copies ran while one was open for 13% of the time, Pallas kernels for 0%

commit v1 on v0

--- a/solution.py
+++ b/solution.py
@@ -10,6 +10,27 @@
 haline = 0.25
 cabbeling = 0.05
 forcing = 4.0
+
+
+def collect(x, axis, dim):
+    size, index, rows = (lax.axis_size(axis), lax.axis_index(axis), x.shape[dim])
+    ahead = [(i, (i + 1) % size) for i in range(size)]
+    downward = [(i, (i - 1) % size) for i in range(size)]
+    filled = jnp.zeros((*x.shape[:dim], size * rows, *x.shape[dim + 1 :]), x.dtype)
+    filled = lax.dynamic_update_slice_in_dim(filled, x, index * rows, axis=dim)
+    from_left = from_right = x
+    half = size // 2
+    for lap in range(1, half + 1):
+        from_left = lax.ppermute(from_left, axis, ahead)
+        filled = lax.dynamic_update_slice_in_dim(
+            filled, from_left, (index - lap) % size * rows, axis=dim
+        )
+        if lap < size - half:
+            from_right = lax.ppermute(from_right, axis, downward)
+            filled = lax.dynamic_update_slice_in_dim(
+                filled, from_right, (index + lap) % size * rows, axis=dim
+            )
+    return filled
 
 
 def passed_along(value, axis, steps):
@@ -195,7 +216,7 @@
     from_below = passed_along(values[:, :, -1, :], "gy", 1)
     from_above = passed_along(values[:, :, 0, :], "gy", -1)
     band_sides, band_below, band_above = (
-        lax.all_gather(side_cols, "gx", axis=1, tiled=True),
+        collect(side_cols, "gx", 1),
         lax.all_gather(from_below, "gx", axis=1, tiled=True),
         lax.all_gather(from_above, "gx", axis=1, tiled=True),
     )

time: 798 us -> 897 us (1.12)
  starting transfers between devices: 36.4 us -> 126 us
  waiting for transfers between devices: 81.1 us -> 115 us
  blocking collectives: 499 us -> 468 us
    ppermute x0 -> x45, starting transfers between devices: none -> 101 us  [the longest x21 98.9 us: collect(): from_right = lax.ppermute(from_right, axis, downward)]
    all_gather x3 -> x0, blocking collectives: 48.3 us -> none  [exchange_edges(): lax.all_gather(side_cols, 'gx', axis=1, tiled=True)]
    ppermute x0 -> x45, waiting for transfers between devices: none -> 33.9 us  [the longest x24 33.8 us: collect(): from_left = lax.ppermute(from_left, axis, ahead)]
    psum x2, blocking collectives: 145 us -> 161 us  [solve(): lax.psum(jnp.sum(direction * image_field), ('gx', 'gy'))]
    ppermute x8, starting transfers between devices: 36.3 us -> 25 us  [passed_along(): lax.ppermute(value, axis, [(source, source + steps) for source in range(l...]
  transfers between devices with their start and end apart: 12 -> 57, of which waited for: 4 -> 25; matrix products, arithmetic and copies ran while one was open for 13% -> 12% of each run, Pallas kernels for 0% -> 0%
where the time goes in v1:
time: 897 us; the launch traced here: 890 us
  blocking collectives  468 us (52%)
  starting transfers between devices  126 us (14%)
  waiting for transfers between devices  115 us (13%)
  local copies, waits for them, and re-layouts  101 us (11%)
  other arithmetic  44.9 us (5%)
  between operations  33.9 us (4%)
    psum x3, blocking collectives, squares(): return lax.psum(jnp.sum(residual * residual), ('gx', 'gy'))  209 us
    psum x2, blocking collectives, solve(): lax.psum(jnp.sum(direction * image_field), ('gx', 'gy'))  161 us
    ppermute x21, starting transfers between devices, collect(): from_right = lax.ppermute(from_right, axis, downward)  98.9 us
    all_gather x3, blocking collectives, exchange_edges(): lax.all_gather(from_above, 'gx', axis=1, tiled=True)  49.5 us
    all_gather x3, blocking collectives, exchange_edges(): lax.all_gather(from_below, 'gx', axis=1, tiled=True)  48.6 us
    ppermute x24, waiting for transfers between devices, collect(): from_left = lax.ppermute(from_left, axis, ahead)  33.8 us
    all_gather x1, waiting for transfers between devices, body(): lax.all_gather(side_cols, 'gx', axis=1, tiled=True)  33.2 us
    all_gather x1, waiting for transfers between devices, body(): band_fields = lax.all_gather(packed, 'gx', axis=1, tiled=True)  30.9 us
  transfers between devices with their start and end apart: 57, of which 25 were waited for; matrix products, arithmetic and copies ran while one was open for 12% of the time, Pallas kernels for 0%

profile of v1, /device:TPU:1, one launch (start us, length us, event | category | flops | bytes accessed | tf_op | source)
XLA Modules:
  0.0 889.5 jit_solution(16863385298930517458)
XLA Ops:
  10.1 7.6 slice_reduce_fusion
  20.7 5.4 constant_dynamic-update-slice_fusion.1
  30.2 6.4 scatter_fusion
  36.6 5.6 fusion.188
  55.8 5.6 fusion.187
  67.7 33.2 %all-gather.5.cloned.1.call-done = f32[1,16,20864]{2,0,1:T(1,128)} async-done(((f32[1,1,20864]{2,0,1:T(1,128)}), f32[1,16,20864]{2,0,1:T(1,128)}) %all-gather.5.cloned.1.call-update) | async-done | bytes 1335312 | tf_op jit(solution)/shard_map/all_gather | solution.py:291
  102.7 6.8 concatenate.612
  109.6 6.9 concatenate.611
  124.6 5.6 multiply_subtract_fusion
  135.6 9.8 %slice_multiply_fusion = (f32[1,1,4,36,64,1]{5,4,3,2,1,0:T(8,128)}, f32[1,1,4,36,64,1]{5,4,3,2,1,0:T(8,128)}) fusion(f32[1,1,4,36,64,129]{5,4,3,2,1,0:T(8,128)} %copy-done, f32[]{:T(128)} %bitcast.22, f32[]{:T(128)} %bitcast.21), kind=kLoop, calls=%fused_computation.25 | loop fusion | flops 18432 | bytes 147464 | tf_op jit(solution)/shard_map/mul | solution.py:93
  152.7 15.5 %collective-permute-done = f32[1,16,23168]{2,0,1:T(1,128)S(1)} collective-permute-done((f32[1,16,23168]{2,0,1:T(1,128)}, f32[1,16,23168]{2,0,1:T(1,128)S(1)}, u32[]{:S(2)}, u32[]{:S(2)}) %collective-permute-start) | collective-permute-done | bytes 1482784 | tf_op jit(solution)/shard_map/ppermute | solution.py:39
  176.5 9.3 %fusion.1 = f32[1,1,4,36,64,128]{5,4,3,2,1,0:T(8,128)S(1)} fusion(f32[1,1,4,36,64,128]{5,4,3,2,1,0:T(8,128)S(1)} %bitcast.768, f32[1,1,4,36,64,1]{5,4,3,2,1,0:T(8,128)} %get-tuple-element.259, f32[1,1,4,36,64,127]{5,4,3,2,1,0:T(8,128)S(1)} %bitcast.770, f32[1,1,4,36,64,1]{5,4,3,2,1,0:T(8,128)} %get-tuple-element.258, ...), kind=kLoop, calls=%fused_computation.29 | loop fusion | flops 9437184 | bytes 18984960 | tf_op jit(solution)/shard_map/sub | solution.py:135
  193.7 11.2 %scatter_fusion.1 = s32[8,29]{1,0:T(8,128)S(1)} fusion(s32[8,29]{1,0:T(8,128)S(1)} %broadcast.10968.clone.1, s32[256]{0:T(256)S(1)} %reshape.20145, s32[256]{0:T(256)S(1)} %reshape.20147), kind=kCustom, calls=%fused_computation.19 | custom fusion | bytes 5120 | tf_op jit(solution)/shard_map/scatter | solution.py:51
  208.7 30.9 %all-gather.11.cloned.1.call-done = f32[1,16,5,64,128]{4,3,2,0,1:T(8,128)} async-done(((f32[1,1,5,64,128]{4,3,2,0,1:T(8,128)}), f32[1,16,5,64,128]{4,3,2,0,1:T(8,128)}) %all-gather.11.cloned.1.call-update) | async-done | bytes 2621456 | tf_op jit(solution)/shard_map/all_gather | solution.py:340
  253.1 15.9 %all_gather.35 = f32[1,32,128]{2,0,1:T(1,128)S(1)} all-gather(f32[1,2,128]{2,0,1:T(1,128)S(1)} %bitcast.804), channel_id=1, replica_groups=mesh['gx'=16,'gy'=8] {'gx'}, dimensions={1}, use_global_device_ids=true | all-gather | bytes 17408 | tf_op jit(solution)/shard_map/all_gather | solution.py:220
  269.0 16.8 %all_gather.34 = f32[1,32,128]{2,0,1:T(1,128)S(1)} all-gather(f32[1,2,128]{2,0,1:T(1,128)S(1)} %bitcast.809), channel_id=1, replica_groups=mesh['gx'=16,'gy'=8] {'gx'}, dimensions={1}, use_global_device_ids=true | all-gather | bytes 17408 | tf_op jit(solution)/shard_map/all_gather | solution.py:221
  316.2 4.8 collective-permute-start.15
  322.0 5.7 collective-permute-done.16
  330.0 81.7 %all-reduce.4 = (f32[]{:T(128)}, f32[]{:T(128)}) all-reduce(f32[]{:T(128)} %get-tuple-element.130, f32[]{:T(128)} %get-tuple-element.129), channel_id=1, replica_groups=mesh['gx'=16,'gy'=8] {'gx','gy'}, use_global_device_ids=true, to_apply=%region_3.5 | all-reduce | flops 2 | bytes 16 | tf_op jit(solution)/shard_map/psum | solution.py:232
  413.6 64.1 %psum.44 = f32[]{:T(128)} all-reduce(f32[]{:T(128)} %get-tuple-element.147), channel_id=1, replica_groups=mesh['gx'=16,'gy'=8] {'gx','gy'}, use_global_device_ids=true, to_apply=%region_8.11 | all-reduce | flops 1 | bytes 8 | tf_op jit(solution)/shard_map/psum | solution.py:232
  489.2 14.9 %all_gather.37 = f32[1,32,128]{2,0,1:T(1,128)S(1)} all-gather(f32[1,2,128]{2,0,1:T(1,128)S(1)} %bitcast.805), channel_id=1, replica_groups=mesh['gx'=16,'gy'=8] {'gx'}, dimensions={1}, use_global_device_ids=true | all-gather | bytes 17408 | tf_op jit(solution)/shard_map/all_gather | solution.py:220
  504.7 17.8 %all_gather.36 = f32[1,32,128]{2,0,1:T(1,128)S(1)} all-gather(f32[1,2,128]{2,0,1:T(1,128)S(1)} %bitcast.807), channel_id=1, replica_groups=mesh['gx'=16,'gy'=8] {'gx'}, dimensions={1}, use_global_device_ids=true | all-gather | bytes 17408 | tf_op jit(solution)/shard_map/all_gather | solution.py:221
  557.6 5.7 collective-permute-done.33
  565.7 81.1 %psum.45 = f32[]{:T(128)} all-reduce(f32[]{:T(128)} %get-tuple-element.143), channel_id=1, replica_groups=mesh['gx'=16,'gy'=8] {'gx','gy'}, use_global_device_ids=true, to_apply=%region_10.13 | all-reduce | flops 1 | bytes 8 | tf_op jit(solution)/shard_map/psum | solution.py:242
  648.7 63.2 %psum.46 = f32[]{:T(128)} all-reduce(f32[]{:T(128)} %multiply_reduce_fusion), channel_id=1, replica_groups=mesh['gx'=16,'gy'=8] {'gx','gy'}, use_global_device_ids=true, to_apply=%region_12.15 | all-reduce | flops 1 | bytes 8 | tf_op jit(solution)/shard_map/psum | solution.py:232
  724.4 14.9 %all_gather.38 = f32[1,32,128]{2,0,1:T(1,128)S(1)} all-gather(f32[1,2,128]{2,0,1:T(1,128)S(1)} %bitcast.808), channel_id=1, replica_groups=mesh['gx'=16,'gy'=8] {'gx'}, dimensions={1}, use_global_device_ids=true | all-gather | bytes 17408 | tf_op jit(solution)/shard_map/all_gather | solution.py:221
  739.9 17.8 %all_gather.39 = f32[1,32,128]{2,0,1:T(1,128)S(1)} all-gather(f32[1,2,128]{2,0,1:T(1,128)S(1)} %bitcast.806), channel_id=1, replica_groups=mesh['gx'=16,'gy'=8] {'gx'}, dimensions={1}, use_global_device_ids=true | all-gather | bytes 17408 | tf_op jit(solution)/shard_map/all_gather | solution.py:220
  775.6 4.8 collective-permute-start.45
  781.4 4.8 collective-permute-start.47
  787.1 4.8 collective-permute-start.49
  792.9 5.7 collective-permute-done.50
  800.9 80.0 %psum.47 = f32[]{:T(128)} all-reduce(f32[]{:T(128)} %fusion.60), channel_id=1, replica_groups=mesh['gx'=16,'gy'=8] {'gx','gy'}, use_global_device_ids=true, to_apply=%region_14.17 | all-reduce | flops 1 | bytes 8 | tf_op jit(solution)/shard_map/psum | solution.py:242
  (463 shorter events, 191.4 us)
Async XLA Ops:
  7.2 57.0 %all-gather.9.cloned.1.call-start = ((), (), s32[]{:S(2)}) async-start(), calls=%async_computation.2 | async-start | bytes 1262080 | tf_op jit(solution)/shard_map/all_gather | solution.py:293
  10.0 90.9 %all-gather.5.cloned.1.call-start = ((), (), s32[]{:S(2)}) async-start(), calls=%async_computation | async-start | bytes 1418752 | tf_op jit(solution)/shard_map/all_gather | solution.py:291
  19.9 127.2 %all-gather.7.cloned.1.call-start = ((), (), s32[]{:S(2)}) async-start(), calls=%async_computation.1 | async-start | bytes 1575424 | tf_op jit(solution)/shard_map/all_gather | solution.py:292
  20.7 218.9 %all-gather.11.cloned.1.call-start = ((), (), s32[]{:S(2)}) async-start(), calls=%async_computation.3 | async-start | bytes 2785280 | tf_op jit(solution)/shard_map/all_gather | solution.py:340
  64.2 87.6 %collective-permute-start.1 = (f32[1,16,18560]{2,0,1:T(1,128)}, f32[1,16,18560]{2,0,1:T(1,128)}, u32[]{:S(2)}, u32[]{:S(2)}) collective-permute-start(f32[1,16,18560]{2,0,1:T(1,128)} %all-gather.9.cloned.1.call-done), channel_id=1, source_target_pairs={{1,0},{2,1},{3,2},{4,3},{5,4},{6,5},{7,6},{9,8},{10,9},{11,10},{12... | collective-permute-start | bytes 3563528 | tf_op jit(solution)/shard_map/ppermute | solution.py:39
  147.1 21.1 %collective-permute-start = (f32[1,16,23168]{2,0,1:T(1,128)}, f32[1,16,23168]{2,0,1:T(1,128)S(1)}, u32[]{:S(2)}, u32[]{:S(2)}) collective-permute-start(f32[1,16,23168]{2,0,1:T(1,128)} %all-gather.7.cloned.1.call-done), channel_id=1, source_target_pairs={{0,1},{1,2},{2,3},{3,4},{4,5},{5,6},{6,7},{8,9},{9,10},{10,11},{11... | collective-permute-start | bytes 4448264 | tf_op jit(solution)/shard_map/ppermute | solution.py:39
  242.3 10.8 %collective-permute-start.18 = (f32[1,2,128]{2,1,0:T(2,128)S(1)}, f32[1,2,128]{2,1,0:T(2,128)S(1)}, u32[]{:S(2)}, u32[]{:S(2)}) collective-permute-start(f32[1,2,128]{2,1,0:T(2,128)S(1)} %bitcast.812), channel_id=1, source_target_pairs={{0,1},{1,2},{2,3},{3,4},{4,5},{5,6},{6,7},{8,9},{9,10},{10,11},{11... | collective-permute-start | bytes 3080 | tf_op jit(solution)/shard_map/ppermute | solution.py:39
  246.4 40.7 %collective-permute-start.2 = (f32[1,2,128]{2,1,0:T(2,128)S(1)}, f32[1,2,128]{2,1,0:T(2,128)S(1)}, u32[]{:S(2)}, u32[]{:S(2)}) collective-permute-start(f32[1,2,128]{2,1,0:T(2,128)S(1)} %get-tuple-element.153), channel_id=1, source_target_pairs={{0,8},{8,16},{16,24},{24,32},{32,40},{40,48},{48,56},{56,64},{64,7... | collective-permute-start | bytes 3080 | tf_op jit(solution)/shard_map/ppermute | solution.py:24
  247.3 39.8 %collective-permute-start.3 = (f32[1,2,128]{2,1,0:T(2,128)S(1)}, f32[1,2,128]{2,1,0:T(2,128)S(1)}, u32[]{:S(2)}, u32[]{:S(2)}) collective-permute-start(f32[1,2,128]{2,1,0:T(2,128)S(1)} %get-tuple-element.153), channel_id=1, source_target_pairs={{0,120},{8,0},{16,8},{24,16},{32,24},{40,32},{48,40},{56,48},{64,5... | collective-permute-start | bytes 3080 | tf_op jit(solution)/shard_map/ppermute | solution.py:29
  251.2 17.8 %collective-permute-start.17 = (f32[1,2,128]{2,1,0:T(2,128)S(1)}, f32[1,2,128]{2,1,0:T(2,128)S(1)}, u32[]{:S(2)}, u32[]{:S(2)}) collective-permute-start(f32[1,2,128]{2,1,0:T(2,128)S(1)} %bitcast.811), channel_id=1, source_target_pairs={{1,0},{2,1},{3,2},{4,3},{5,4},{6,5},{7,6},{9,8},{10,9},{11,10},{12... | collective-permute-start | bytes 3080 | tf_op jit(solution)/shard_map/ppermute | solution.py:39
  287.1 5.8 collective-permute-start.4
  292.8 5.7 collective-permute-start.6
  292.8 5.7 collective-permute-start.7
  298.6 5.7 collective-permute-start.8
  298.6 5.7 collective-permute-start.9
  304.3 5.7 collective-permute-start.10
  304.3 6.1 collective-permute-start.11
  310.1 6.1 collective-permute-start.12
  316.2 5.7 collective-permute-start.14
  316.2 5.7 collective-permute-start.15
  321.9 5.7 collective-permute-start.16
  479.4 9.8 %collective-permute-start.35 = (f32[1,2,128]{2,1,0:T(2,128)S(1)}, f32[1,2,128]{2,1,0:T(2,128)S(1)}, u32[]{:S(2)}, u32[]{:S(2)}) collective-permute-start(f32[1,2,128]{2,1,0:T(2,128)S(1)} %bitcast.813), channel_id=1, source_target_pairs={{0,1},{1,2},{2,3},{3,4},{4,5},{5,6},{6,7},{8,9},{9,10},{10,11},{11... | collective-permute-start | bytes 3080 | tf_op jit(solution)/shard_map/ppermute | solution.py:39
  481.8 41.4 %collective-permute-start.19 = (f32[1,2,128]{2,1,0:T(2,128)S(1)}, f32[1,2,128]{2,1,0:T(2,128)S(1)}, u32[]{:S(2)}, u32[]{:S(2)}) collective-permute-start(f32[1,2,128]{2,1,0:T(2,128)S(1)} %get-tuple-element.146), channel_id=1, source_target_pairs={{0,8},{8,16},{16,24},{24,32},{32,40},{40,48},{48,56},{56,64},{64,7... | collective-permute-start | bytes 3080 | tf_op jit(solution)/shard_map/ppermute | solution.py:24
  482.2 41.0 %collective-permute-start.20 = (f32[1,2,128]{2,1,0:T(2,128)S(1)}, f32[1,2,128]{2,1,0:T(2,128)S(1)}, u32[]{:S(2)}, u32[]{:S(2)}) collective-permute-start(f32[1,2,128]{2,1,0:T(2,128)S(1)} %get-tuple-element.146), channel_id=1, source_target_pairs={{0,120},{8,0},{16,8},{24,16},{32,24},{40,32},{48,40},{56,48},{64,5... | collective-permute-start | bytes 3080 | tf_op jit(solution)/shard_map/ppermute | solution.py:29
  486.5 18.1 %collective-permute-start.34 = (f32[1,2,128]{2,1,0:T(2,128)S(1)}, f32[1,2,128]{2,1,0:T(2,128)S(1)}, u32[]{:S(2)}, u32[]{:S(2)}) collective-permute-start(f32[1,2,128]{2,1,0:T(2,128)S(1)} %bitcast.810), channel_id=1, source_target_pairs={{1,0},{2,1},{3,2},{4,3},{5,4},{6,5},{7,6},{9,8},{10,9},{11,10},{12... | collective-permute-start | bytes 3080 | tf_op jit(solution)/shard_map/ppermute | solution.py:39
  523.2 5.8 collective-permute-start.21
  528.9 5.7 collective-permute-start.23
  713.4 45.0 %collective-permute-start.36 = (f32[1,2,128]{2,1,0:T(2,128)S(1)}, f32[1,2,128]{2,1,0:T(2,128)S(1)}, u32[]{:S(2)}, u32[]{:S(2)}) collective-permute-start(f32[1,2,128]{2,1,0:T(2,128)S(1)} %get-tuple-element.142), channel_id=1, source_target_pairs={{0,8},{8,16},{16,24},{24,32},{32,40},{40,48},{48,56},{56,64},{64,7... | collective-permute-start | bytes 3080 | tf_op jit(solution)/shard_map/ppermute | solution.py:24
  713.7 44.7 %collective-permute-start.37 = (f32[1,2,128]{2,1,0:T(2,128)S(1)}, f32[1,2,128]{2,1,0:T(2,128)S(1)}, u32[]{:S(2)}, u32[]{:S(2)}) collective-permute-start(f32[1,2,128]{2,1,0:T(2,128)S(1)} %get-tuple-element.142), channel_id=1, source_target_pairs={{0,120},{8,0},{16,8},{24,16},{32,24},{40,32},{48,40},{56,48},{64,5... | collective-permute-start | bytes 3080 | tf_op jit(solution)/shard_map/ppermute | solution.py:29
  718.3 6.1 collective-permute-start.51
  721.5 18.5 %collective-permute-start.52 = (f32[1,2,128]{2,1,0:T(2,128)S(1)}, f32[1,2,128]{2,1,0:T(2,128)S(1)}, u32[]{:S(2)}, u32[]{:S(2)}) collective-permute-start(f32[1,2,128]{2,1,0:T(2,128)S(1)} %bitcast.814), channel_id=1, source_target_pairs={{0,1},{1,2},{2,3},{3,4},{4,5},{5,6},{6,7},{8,9},{9,10},{10,11},{11... | collective-permute-start | bytes 3080 | tf_op jit(solution)/shard_map/ppermute | solution.py:39
  758.4 5.8 collective-permute-start.38
  (78 other events, 629.7 us)
Sparse Core Ops, SparseCore 0:
  10.1 45.2 all-gather.8
  58.2 42.6 all-gather.4
  103.1 43.9 all-gather.6
  193.6 45.9 all-gather.10
